TPU v7x, 256 devices: a whole 4x4x8 slice. The times are simulated.
256 devices in a mesh: row: 32 (over z_hi, y, core), col: 8 (over z_lo, x).
Axes of the slice: x: 4, y: 4, z: 8 (z_hi: 4, z_lo: 2; z = z_hi * 2 + z_lo), core: 2. Of those that a mesh axis runs over, the one named last changes fastest.
Arguments:
- known_inverse: float32 [20480, 20480], P('row', 'col'), may hold values from -1.7818667 to 1.7818667, as said below
- first_panel: float32 [20480, 512], P('col', 'row'), may hold values from -1.25 to 1.25
- second_panel: float32 [20480, 512], P('col', 'row'), may hold values from -1.25 to 1.25
- coupling: float32 [512, 512], replicated, may hold values from -0.25 to 0.25
- first_diag: float32 [512, 512], replicated, may hold values from -6 to 6
- second_diag: float32 [512, 512], replicated, may hold values from -6 to 6
- first_present: int32 [160], replicated, may hold values 0 or 1
- second_present: int32 [160], replicated, may hold values 0 or 1
Outputs:
- first_block: float32 [20480, 512], P(('row', 'col'))
- first_inverse_diag: float32 [512, 512], P(None, 'col')
- second_block: float32 [20480, 512], P(('row', 'col'))
- second_cross: float32 [512, 512], P(None, 'col')
- second_inverse_diag: float32 [512, 512], P(None, 'col')
Inputs may be any that keep to these rules, and one draw needn't show every extreme that they name: known_inverse is exactly symmetric.
All inputs are finite; a program needn't handle non-finite values.
Results may differ from a plain program's by a relative error of at most 0.000098.
Values sent between devices are 32-bit elements; how exact they have to be, the bound alone decides.
A program may use at most 64 MiB of HBM per device.

v0:
```python
import jax
import jax.numpy as jnp
from jax import lax
from jax.sharding import PartitionSpec as P

BLK = 128


def spread(block, axis, holder):
    block = jnp.where(lax.axis_index(axis) == holder, block, jnp.zeros_like(block))
    return lax.psum(block, axis)


def product(left, right):
    return jnp.dot(left, right, precision=lax.Precision.HIGHEST, preferred_element_type=jnp.float32)


def transposed(left, right):
    return lax.dot_general(
        left,
        right,
        (((0,), (0,)), ((), ())),
        precision=lax.Precision.HIGHEST,
        preferred_element_type=jnp.float32,
    )


def masked(panel, present, col_index):
    row_total, col_total = panel.shape
    blocks = row_total // BLK
    local = lax.dynamic_slice_in_dim(present, col_index * blocks, blocks)
    shaped = panel.reshape(blocks, BLK, col_total) * local.astype(jnp.float32)[:, None, None]
    return shaped.reshape(row_total, col_total)


def piece_products(known_inverse, column_one, column_two, piece_one, piece_two, coupling):
    first_block = -lax.psum_scatter(
        product(known_inverse, column_one), "col", scatter_dimension=0, tiled=True
    )
    reached = lax.psum_scatter(
        product(known_inverse, column_two), "col", scatter_dimension=0, tiled=True
    )
    first_partial = transposed(piece_one, first_block)
    second_block = -(reached + product(first_block, coupling))
    cross_partial = transposed(first_block, piece_two)
    diag_partial = transposed(piece_two, second_block)
    return (first_block, second_block, first_partial, cross_partial, diag_partial)


def on_device(
    known_inverse,
    first_panel,
    second_panel,
    coupling,
    first_diag,
    second_diag,
    first_present,
    second_present,
):
    col_count = lax.axis_size("col")
    row_index = lax.axis_index("row")
    col_index = lax.axis_index("col")
    local_one = masked(first_panel, first_present, col_index)
    local_two = masked(second_panel, second_present, col_index)
    column_one, column_two = (
        lax.all_gather(local_one, "row", axis=1, tiled=True),
        lax.all_gather(local_two, "row", axis=1, tiled=True),
    )
    band_rows = known_inverse.shape[0]
    block_cols = known_inverse.shape[1]
    piece_rows = band_rows // col_count
    width_total = coupling.shape[0]
    owner = row_index * band_rows // block_cols
    offset = row_index * band_rows % block_cols
    own_start = col_index * piece_rows
    band_one = lax.dynamic_slice_in_dim(column_one, offset, band_rows)
    band_two = lax.dynamic_slice_in_dim(column_two, offset, band_rows)
    band_one, band_two = (spread(band_one, "col", owner), spread(band_two, "col", owner))
    piece_one = lax.dynamic_slice_in_dim(band_one, own_start, piece_rows)
    piece_two = lax.dynamic_slice_in_dim(band_two, own_start, piece_rows)
    first_block, second_block, first_partial, cross_partial, diag_partial = piece_products(
        known_inverse, column_one, column_two, piece_one, piece_two, coupling
    )
    col_width = width_total // col_count
    col_start = col_index * col_width
    first_sum = lax.psum(first_partial, ("row", "col"))
    first_inverse_diag = first_diag - first_sum
    cross_sum, diag_sum = lax.psum((cross_partial, diag_partial), ("row", "col"))
    second_cross = -(cross_sum + product(first_inverse_diag, coupling))
    second_inverse_diag = second_diag - diag_sum - transposed(coupling, second_cross)
    first_out = lax.dynamic_slice_in_dim(first_inverse_diag, col_start, col_width, 1)
    cross_out = lax.dynamic_slice_in_dim(second_cross, col_start, col_width, 1)
    second_out = lax.dynamic_slice_in_dim(second_inverse_diag, col_start, col_width, 1)
    return (first_block, first_out, second_block, cross_out, second_out)


def solution(mesh):
    in_specs = (P("row", "col"), P("col", "row"), P("col", "row"), P(), P(), P(), P(), P())
    out_specs = (
        P(("row", "col"), None),
        P(None, "col"),
        P(("row", "col"), None),
        P(None, "col"),
        P(None, "col"),
    )
    return jax.shard_map(
        on_device, mesh=mesh, in_specs=in_specs, out_specs=out_specs, check_vma=False
    )
```

profile of v0, /device:TPU:1, one launch (start us, length us, event | category | flops | bytes accessed | tf_op | source)
XLA Modules:
  0.0 610.7 jit_solution(1774505497310201889)
XLA Ops:
  7.2 0.0 copy-start
  7.2 0.0 all-gather.3.cloned.1.call-start
  7.2 0.9 dynamic-slice_convert_fusion
  8.1 0.1 broadcast_bitcast_fusion.1
  8.2 1.6 broadcast_multiply_fusion.1
  9.8 0.0 all-gather.3.cloned.1.call-update
  9.8 0.0 all-gather.5.cloned.1.call-start
  9.8 0.1 broadcast_bitcast_fusion
  9.9 1.6 broadcast_multiply_fusion
  11.5 0.0 all-gather.5.cloned.1.call-update
  11.5 0.0 reduce-scatter.7.cloned.1.call-start
  11.6 68.0 %all-gather.3.cloned.1.call-done = f32[2560,512]{0,1:T(8,128)} async-done(((f32[2560,16]{0,1:T(8,128)}), f32[2560,512]{0,1:T(8,128)}) %all-gather.3.cloned.1.call-update) | async-done | bytes 5242896 | tf_op jit(solution)/shard_map/all_gather | solution.py:66
  79.6 15.7 %convolution_bitcast_fusion.1 = f32[640,512]{0,1:T(8,128)S(1)} fusion(f32[2560,512]{0,1:T(8,128)} %all-gather.3.cloned.1.call-done, f32[640,2560]{1,0:T(8,128)} %param.8), kind=kOutput, calls=%fused_computation.1 | convolution fusion | flops 10066329600 | bytes 13107200 | tf_op jit(solution)/shard_map/dot_general | solution.py:15
  95.4 1.5 copy.27
  96.8 0.0 reduce-scatter.7.cloned.1.call-update
  96.8 0.0 all-reduce.7.cloned.1.call-start
  96.9 2.9 dynamic-slice_select_fusion.1
  99.9 45.0 %all-gather.5.cloned.1.call-done = f32[2560,512]{0,1:T(8,128)} async-done(((f32[2560,16]{0,1:T(8,128)}), f32[2560,512]{0,1:T(8,128)}) %all-gather.5.cloned.1.call-update) | async-done | bytes 5242896 | tf_op jit(solution)/shard_map/all_gather | solution.py:67
  144.9 3.0 dynamic-slice_select_fusion
  147.9 0.0 all-reduce.7.cloned.1.call-update
  147.9 0.2 reduce-scatter.9.cloned.1.call-start
  148.1 15.7 %convolution_bitcast_fusion = f32[640,512]{0,1:T(8,128)S(1)} fusion(f32[2560,512]{0,1:T(8,128)} %all-gather.5.cloned.1.call-done, f32[640,2560]{1,0:T(8,128)} %param.8), kind=kOutput, calls=%fused_computation | convolution fusion | flops 10066329600 | bytes 13107200 | tf_op jit(solution)/shard_map/dot_general | solution.py:15
  163.9 1.5 copy.29
  165.4 0.0 reduce-scatter.9.cloned.1.call-update
  165.4 0.3 all-reduce.5.cloned.1.call-start
  165.7 17.2 %reduce-scatter.7.cloned.1.call-done = f32[80,512]{1,0:T(8,128)} async-done(((f32[640,512]{1,0:T(8,128)}), f32[80,512]{1,0:T(8,128)}) %reduce-scatter.7.cloned.1.call-update) | async-done | bytes 163856
  182.8 1.0 copy.28
  183.9 92.5 %all-reduce.7.cloned.1.call-done = (f32[640,512]{0,1:T(8,128)}, f32[640,512]{0,1:T(8,128)}) async-done(((f32[640,512]{0,1:T(8,128)}, f32[640,512]{0,1:T(8,128)}), (f32[640,512]{0,1:T(8,128)}, f32[640,512]{0,1:T(8,128)})) %all-reduce.7.cloned.1.call-update) | async-done | bytes 2621456 | tf_op jit(solution)/shard_map/psum | solution.py:11
  276.3 3.1 fusion.2
  279.5 3.1 fusion.6
  282.6 37.6 %reduce-scatter.9.cloned.1.call-done = f32[80,512]{1,0:T(8,128)} async-done(((f32[640,512]{1,0:T(8,128)}), f32[80,512]{1,0:T(8,128)}) %reduce-scatter.9.cloned.1.call-update) | async-done | bytes 163856 | tf_op jit(solution)/shard_map/reduce_scatter | solution.py:40
  320.1 0.0 copy-done
  320.1 1.6 fusion.1
  321.8 0.0 copy-start.3
  321.8 3.2 fusion.4
  325.0 0.0 all-reduce.5.cloned.1.call-update
  325.0 0.0 copy-done.3
  325.0 0.0 copy-start.1
  325.0 1.2 constant_dynamic-slice_fusion
  326.2 0.1 copy.31
  326.4 0.8 copy.23
  327.1 268.1 %all-reduce.5.cloned.1.call-done = (f32[512,512]{1,0:T(8,128)}, f32[512,512]{1,0:T(8,128)}, f32[512,512]{0,1:T(8,128)}) async-done(((f32[512,512]{1,0:T(8,128)}, f32[512,512]{1,0:T(8,128)}, f32[512,512]{0,1:T(8,128)}), (f32[512,512]{1,0:T(8,128)}, f32[512,512]{1,0:T(8,128)}, f32[512,512]{0,1:T(8,128)})) %all-reduce.5.cloned.1.call-update) | async-done | bytes 3145744 | tf_op jit(solution)/shard_map/psum | solution.py:86
  595.2 0.0 copy-done.1
  595.2 0.0 copy-start.2
  595.2 1.5 sub.14
  596.7 0.1 constant_dynamic-slice_fusion.2
  596.9 0.0 copy-done.2
  596.9 1.8 fusion
  598.8 0.1 constant_dynamic-slice_fusion.1
  598.9 1.8 convolution_bitcast_fusion.2
  600.8 0.8 copy.24
  601.5 0.8 copy.25
  602.3 1.6 dynamic-slice_subtract_fusion
  (1 shorter events, 0.0 us)
Async XLA Ops:
  7.2 313.0 %copy-start = (f32[512,512]{1,0:T(8,128)S(1)}, f32[512,512]{1,0:T(8,128)}, u32[]{:S(2)}) copy-start(f32[512,512]{1,0:T(8,128)} %param.11) | copy-start | bytes 3145732
  7.2 72.4 %all-gather.3.cloned.1.call-start = ((), (), s32[]{:S(2)}) async-start(), calls=%async_computation.2 | async-start | bytes 5406720 | tf_op jit(solution)/shard_map/all_gather | solution.py:66
  9.8 135.1 %all-gather.5.cloned.1.call-start = ((), (), s32[]{:S(2)}) async-start(), calls=%async_computation.3 | async-start | bytes 5406720 | tf_op jit(solution)/shard_map/all_gather | solution.py:67
  11.5 171.3 %reduce-scatter.7.cloned.1.call-start = ((), (), s32[]{:S(2)}) async-start(), calls=%async_computation.4 | async-start | bytes 1474560
  96.8 179.5 %all-reduce.7.cloned.1.call-start = ((), (), s32[]{:S(2)}) async-start(), calls=%async_computation.7 | async-start | bytes 5242880 | tf_op jit(solution)/shard_map/psum | solution.py:11
  147.9 172.2 %reduce-scatter.9.cloned.1.call-start = ((), (), s32[]{:S(2)}) async-start(), calls=%async_computation.5 | async-start | bytes 1474560 | tf_op jit(solution)/shard_map/reduce_scatter | solution.py:40
  165.4 429.8 %all-reduce.5.cloned.1.call-start = ((), (), s32[]{:S(2)}) async-start(), calls=%async_computation.6 | async-start | bytes 6291456 | tf_op jit(solution)/shard_map/psum | solution.py:86
  321.8 3.2 copy-start.3
  325.0 270.2 %copy-start.1 = (f32[512,512]{1,0:T(8,128)S(1)}, f32[512,512]{1,0:T(8,128)}, u32[]{:S(2)}) copy-start(f32[512,512]{1,0:T(8,128)} %param.12) | copy-start | bytes 3145732
  595.2 1.7 copy-start.2
Sparse Core Ops, SparseCore 0:
  11.1 68.4 all-gather.2
  82.7 62.1 all-gather.4
  147.5 35.3 reduce-scatter.6
  185.4 90.8 all-reduce.6
  278.7 41.3 reduce-scatter.8
  325.8 269.4 all-reduce.4
where the time goes:
time: 612 us; the launch traced here: 611 us
  waiting for transfers between devices  528 us (86%)
  matrix products  46.2 us (8%)
  between operations  14.3 us (2%)
  other arithmetic  13.1 us (2%)
  local copies, waits for them, and re-layouts  8.01 us (1%)
    psum x1, waiting for transfers between devices, on_device(): first_sum = lax.psum(first_partial, ('row', 'col'))  268 us
    psum x1, waiting for transfers between devices, spread(): return lax.psum(block, axis)  92.5 us
    all_gather x1, waiting for transfers between devices, on_device(): lax.all_gather(local_one, 'row', axis=1, tiled=True)  68 us
    all_gather x1, waiting for transfers between devices, on_device(): lax.all_gather(local_two, 'row', axis=1, tiled=True)  45 us
    reduce_scatter x1, waiting for transfers between devices, piece_products(): lax.psum_scatter(product(known_inverse, column_two), 'col', scatter_dimen...  37.6 us
    dot_general x4, matrix products, product(): jnp.dot(left, right, precision=lax.Precision.HIGHEST, preferred_element_t...  35 us
    unnamed x7, waiting for transfers between devices  17.3 us
  transfers between devices with their start and end apart: 6, of which 6 were waited for; matrix products, arithmetic and copies ran while one was open for 8% of the time, Pallas kernels for 0%

commit v1 on v0

v1 whole, which is shorter than its diff:
```python
import functools

import jax
import jax.numpy as jnp
from jax import lax
from jax.experimental import pallas as pl
from jax.experimental.pallas import tpu as pltpu
from jax.sharding import PartitionSpec as P

BLK = 128
MESH = pl.DeviceIdType.MESH
F32 = jnp.float32
BF16 = jnp.bfloat16
KSTEP = 512


def split(x):
    hi = x.astype(BF16)
    return hi, (x - hi.astype(F32)).astype(BF16)


def dot3(left, right, dims):
    lh, ll = split(left)
    rh, rl = split(right)
    g = functools.partial(lax.dot_general, dimension_numbers=(dims, ((), ())), preferred_element_type=F32)
    return g(lh, rh) + (g(lh, rl) + g(ll, rh))


class Sends:
    def __init__(self, sems):
        self.sems = sems
        self.started = []

    def __call__(self, src, dst, recv, device):
        copy = pltpu.make_async_remote_copy(
            src_ref=src, dst_ref=dst, send_sem=self.sems.at[len(self.started)], recv_sem=recv,
            device_id=device, device_id_type=MESH,
        )
        copy.start()
        self.started.append(copy)
        return copy

    def finish(self):
        for copy in self.started:
            copy.wait_send()


def panel_kernel(
    k_hbm, one_hbm, two_hbm, coupling, present_one, present_two,
    x1_out, x2_out, p80_out,
    k_f32, k_hi, k_lo, panels, mask, y, from_x, half_out, half_in, own, turned, y_two,
    local_sem, send_sem, recv_sem, x_sem, z_sem, p_send, p_recv,
):
    row = lax.axis_index("row")
    col = lax.axis_index("col")
    g0, y0, k0 = row // 8, (row // 2) % 4, row % 2
    z0, x0 = col // 4, col % 4

    def at(g, yy, k):
        return ((g % 4) * 8 + (yy % 4) * 2 + k, col)

    y_up, y_down = at(g0, y0 + 1, k0), at(g0, y0 + 3, k0)
    g_up, g_down = at(g0 + 1, y0, k0), at(g0 + 3, y0, k0)
    sibling = at(g0, y0, 1 - k0)
    x_mate = [(row, z0 * 4 + (x0 + d) % 4) for d in (1, 2, 3)]
    z_mate = (row, (1 - z0) * 4 + x0)
    p_target = (col * 4 + row // 8, row % 8)
    p_source = ((row % 4) * 8 + col, row // 4)
    stays = jnp.logical_and(p_target[0] == row, p_target[1] == col)

    k_copy = pltpu.make_async_copy(k_hbm, k_f32, local_sem.at[0])
    k_copy.start()
    firsts = [
        pltpu.make_async_copy(one_hbm, panels.at[g0, 0, y0, k0], local_sem.at[1]),
        pltpu.make_async_copy(two_hbm, panels.at[g0, 1, y0, k0], local_sem.at[2]),
    ]
    for copy in firsts:
        copy.start()

    barrier = pltpu.get_barrier_semaphore()
    for device in (y_up, y_down, g_up, g_down, sibling, *x_mate, z_mate):
        pl.semaphore_signal(barrier, inc=1, device_id=device, device_id_type=MESH)

    @pl.when(jnp.logical_not(stays))
    def _():
        pl.semaphore_signal(barrier, inc=1, device_id=p_target, device_id_type=MESH)
        pl.semaphore_signal(barrier, inc=1, device_id=p_source, device_id_type=MESH)

    pl.semaphore_wait(barrier, jnp.where(stays, 9, 11))
    for copy in firsts:
        copy.wait()

    send = Sends(send_sem)

    def part(g, p, yy, k):
        return panels.at[g % 4, p, yy % 4, k]

    def push(g, p, yy, k, device):
        ref = part(g, p, yy, k)
        send(ref, ref, recv_sem.at[g % 4, p, yy % 4, k], device)

    def arrive(g, p, yy, k):
        ref = part(g, p, yy, k)
        pltpu.make_async_remote_copy(
            src_ref=ref, dst_ref=ref, send_sem=send_sem.at[0], recv_sem=recv_sem.at[g % 4, p, yy % 4, k],
            device_id=sibling, device_id_type=MESH,
        ).wait_recv()

    def spread_y(g):
        for p in (0, 1):
            push(g, p, y0, k0, y_up)
            push(g, 1 - p, y0, k0, y_down)
        push(g, 0, y0, k0, sibling)
        push(g, 1, y0, k0, sibling)

    def relay_y(g):
        arrive(g, 0, y0 + 3, k0)
        push(g, 0, y0 + 3, k0, y_up)
        push(g, 0, y0 + 3, k0, sibling)
        arrive(g, 1, y0 + 1, k0)
        push(g, 1, y0 + 1, k0, y_down)
        push(g, 1, y0 + 1, k0, sibling)
        arrive(g, 1, y0 + 3, k0)
        push(g, 1, y0 + 3, k0, sibling)
        arrive(g, 0, y0 + 1, k0)
        push(g, 0, y0 + 1, k0, sibling)

    def end_y(g):
        for p in (0, 1):
            arrive(g, p, y0 + 2, k0)
            push(g, p, y0 + 2, k0, sibling)

    def compute(t, g):
        for yy in range(4):
            for p in (0, 1):
                arrive(g, p, y0 + yy, 1 - k0)
        group = g % 4
        y_ref = y.at[t]

        def step(i, carry):
            lanes = pl.ds(pl.multiple_of(i * KSTEP, KSTEP), KSTEP)
            block = panels[group, :, :, :, :, lanes].reshape(2, 16, 8, KSTEP)
            block = (block * mask[:, :, lanes][:, None]).reshape(256, KSTEP)
            ph, plo = split(block)
            kh, kl = k_hi[:, lanes], k_lo[:, lanes]
            dims = (((1,), (1,)), ((), ()))
            g2 = functools.partial(lax.dot_general, dimension_numbers=dims, preferred_element_type=F32)
            total = (g2(kh, ph) + g2(kl, ph) + g2(kh, plo)).reshape(2, 4, 80, 256)

            @pl.when(i == 0)
            def _():
                y_ref[...] = total

            @pl.when(i > 0)
            def _():
                y_ref[...] += total

            return carry

        lax.fori_loop(0, 2560 // KSTEP, step, 0)
        for d in (1, 2, 3):
            send(y.at[t, :, (x0 + d) % 4], from_x.at[t, d - 1], x_sem.at[t, d - 1], x_mate[d - 1])
        start = jnp.minimum((row * 80) // BLK, 2560 // BLK - 2) * BLK
        lanes = pl.ds(pl.multiple_of(start, BLK), 256)
        window = panels[group, :, :, :, :, lanes].reshape(2, 16, 8, 256)
        window = (window * mask[:, :, lanes][:, None]).reshape(256, 256)
        turned[t] = window.T
        piece = turned.at[t, pl.ds(pl.multiple_of(row * 80 - start, 8), 80)]

        @pl.when(stays)
        def _():
            copy = pltpu.make_async_copy(piece, p80_out.at[group], local_sem.at[3])
            copy.start()
            copy.wait()

        @pl.when(jnp.logical_not(stays))
        def _():
            pltpu.make_async_remote_copy(
                src_ref=piece, dst_ref=p80_out.at[group], send_sem=p_send.at[t], recv_sem=p_recv.at[group],
                device_id=p_target, device_id_type=MESH,
            ).start()

    def reduce_x(t):
        for d in range(3):
            pltpu.make_async_remote_copy(
                src_ref=from_x.at[t, d], dst_ref=from_x.at[t, d], send_sem=send_sem.at[0], recv_sem=x_sem.at[t, d],
                device_id=sibling, device_id_type=MESH,
            ).wait_recv()

        def total(z):
            return y[t, z, x0] + from_x[t, 0, z] + from_x[t, 1, z] + from_x[t, 2, z]

        half_out[t] = total(1 - z0)
        send(half_out.at[t], half_in.at[t], z_sem.at[t], z_mate)
        own[t] = total(z0)

    def finish_y(t, g):
        pltpu.make_async_remote_copy(
            src_ref=half_in.at[t], dst_ref=half_in.at[t], send_sem=send_sem.at[0], recv_sem=z_sem.at[t],
            device_id=sibling, device_id_type=MESH,
        ).wait_recv()
        done = own[t] + half_in[t]
        lanes = pl.ds(pl.multiple_of((g % 4) * BLK, BLK), BLK)
        x1_out[:, lanes] = -done[:, :BLK]
        y_two[:, lanes] = done[:, BLK:]

    order = (g0, g0 + 1, g0 + 3, g0 + 2)

    for p in (0, 1):
        push(g0, p, y0, k0, y_up)
        push(g0, 1 - p, y0, k0, y_down)
        push(g0, p, y0, k0, g_up)
        push(g0, 1 - p, y0, k0, g_down)
        push(g0, p, y0, k0, sibling)

    for p, present in ((0, present_one), (1, present_two)):
        for j in range(2560 // BLK):
            value = present[col * (2560 // BLK) + j].astype(F32)
            mask[p, :, j * BLK:(j + 1) * BLK] = jnp.full((8, BLK), value, F32)
    k_copy.wait()

    def split_rows(i, carry):
        rows = pl.ds(pl.multiple_of(i * 32, 32), 32)
        hi, lo = split(k_f32[rows, :])
        k_hi[rows, :] = hi
        k_lo[rows, :] = lo
        return carry

    lax.fori_loop(0, 20, split_rows, 0)

    relay_y(order[0])
    arrive(g0 + 3, 0, y0, k0)
    push(g0 + 3, 0, y0, k0, g_up)
    arrive(g0 + 1, 1, y0, k0)
    push(g0 + 1, 1, y0, k0, g_down)
    end_y(order[0])
    arrive(g0 + 1, 0, y0, k0)
    spread_y(order[1])
    compute(0, order[0])
    relay_y(order[1])
    arrive(g0 + 3, 1, y0, k0)
    spread_y(order[2])
    end_y(order[1])
    compute(1, order[1])
    reduce_x(0)
    relay_y(order[2])
    arrive(g0 + 2, 0, y0, k0)
    arrive(g0 + 2, 1, y0, k0)
    spread_y(order[3])
    end_y(order[2])
    compute(2, order[2])
    reduce_x(1)
    finish_y(0, order[0])
    relay_y(order[3])
    end_y(order[3])
    compute(3, order[3])
    reduce_x(2)
    finish_y(1, order[1])
    reduce_x(3)
    finish_y(2, order[2])
    finish_y(3, order[3])
    x2_out[...] = -(y_two[...] + dot3(x1_out[...], coupling[...], ((1,), (0,))))

    send.finish()

    @pl.when(jnp.logical_not(stays))
    def _():
        for t in range(4):
            copy = pltpu.make_async_remote_copy(
                src_ref=turned.at[t, pl.ds(0, 80)], dst_ref=p80_out.at[t], send_sem=p_send.at[t],
                recv_sem=p_recv.at[t], device_id=p_target, device_id_type=MESH,
            )
            copy.wait_send()
            copy.wait_recv()


def panel_stage(known_inverse, one, two, coupling, present_one, present_two):
    vmem = pl.BlockSpec(memory_space=pltpu.VMEM)
    hbm = pl.BlockSpec(memory_space=pl.ANY)
    smem = pl.BlockSpec(memory_space=pltpu.SMEM)
    dma = pltpu.SemaphoreType.DMA
    return pl.pallas_call(
        panel_kernel,
        out_shape=(
            jax.ShapeDtypeStruct((80, 512), F32),
            jax.ShapeDtypeStruct((80, 512), F32),
            jax.ShapeDtypeStruct((4, 80, 256), F32),
        ),
        in_specs=[hbm, hbm, hbm, vmem, smem, smem],
        out_specs=(vmem, vmem, vmem),
        scratch_shapes=[
            pltpu.VMEM((640, 2560), F32),
            pltpu.VMEM((640, 2560), BF16),
            pltpu.VMEM((640, 2560), BF16),
            pltpu.VMEM((4, 2, 4, 2, 16, 2560), F32),
            pltpu.VMEM((2, 8, 2560), F32),
            pltpu.VMEM((4, 2, 4, 80, 256), F32),
            pltpu.VMEM((4, 3, 2, 80, 256), F32),
            pltpu.VMEM((4, 80, 256), F32),
            pltpu.VMEM((4, 80, 256), F32),
            pltpu.VMEM((4, 80, 256), F32),
            pltpu.VMEM((4, 256, 256), F32),
            pltpu.VMEM((80, 512), F32),
            dma((4,)),
            dma((82,)),
            dma((4, 2, 4, 2)),
            dma((4, 3)),
            dma((4,)),
            dma((4,)),
            dma((4,)),
        ],
        compiler_params=pltpu.CompilerParams(
            collective_id=0, has_side_effects=True, vmem_limit_bytes=56 * 2**20
        ),
        name="panels",
    )(known_inverse, one, two, coupling, present_one, present_two)


def dot_high(left, right, dims):
    return lax.dot_general(left, right, (dims, ((), ())), precision=lax.Precision.HIGH, preferred_element_type=F32)


def on_device(known_inverse, first_panel, second_panel, coupling, first_diag, second_diag, first_present, second_present):
    x1, x2, p80 = panel_stage(known_inverse, first_panel.T, second_panel.T, coupling, first_present, second_present)
    p = p80.reshape(4, 80, 2, 128).transpose(2, 1, 0, 3).reshape(2, 80, 512)
    rows = ((0,), (0,))
    sums = jnp.stack([dot_high(x1, p[0], rows), dot_high(x2, p[0], rows), dot_high(x2, p[1], rows)], axis=1)
    mine = lax.psum_scatter(sums, "col", scatter_dimension=0, tiled=True)
    mine = lax.psum(mine, "row")
    start = lax.axis_index("col") * 64
    diag_one = lax.dynamic_slice_in_dim(first_diag, start, 64, 1)
    diag_two = lax.dynamic_slice_in_dim(second_diag, start, 64, 1)
    coupling_part = lax.dynamic_slice_in_dim(coupling, start, 64, 1)
    first_out = diag_one - mine[:, 0].T
    cross = -mine[:, 1].T - dot_high(first_diag, coupling_part, ((1,), (0,)))
    second_out = diag_two - mine[:, 2].T - dot_high(coupling, cross, ((0,), (0,)))
    return x1, first_out, x2, cross, second_out


def solution(mesh):
    in_specs = (P("row", "col"), P("col", "row"), P("col", "row"), P(), P(), P(), P(), P())
    out_specs = (P(("row", "col"), None), P(None, "col"), P(("row", "col"), None), P(None, "col"), P(None, "col"))
    return jax.shard_map(on_device, mesh=mesh, in_specs=in_specs, out_specs=out_specs, check_vma=False)
```

time: 612 us -> 458 us (0.75)
  waiting for transfers between devices: 528 us -> 327 us
  Pallas kernels: 0 us -> 101 us
  matrix products: 46.2 us -> 6.48 us
  other arithmetic: 13.1 us -> 3.57 us
    all_gather x2 -> x0, waiting for transfers between devices: 113 us -> none  [the longest x1 68 us: on_device(): lax.all_gather(local_one, 'row', axis=1, tiled=True)]
    pallas_call x0 -> x1, Pallas kernels: none -> 101 us  [panel_stage(): pl.pallas_call(panel_kernel, out_shape=(jax.ShapeDtypeStruct((80, 512), F...]
    psum x2 -> x1, waiting for transfers between devices: 361 us -> 281 us  [on_device(): mine = lax.psum(mine, 'row')]
    dot_general x8 -> x5, matrix products: 46.2 us -> 6.48 us  [dot_high(): lax.dot_general(left, right, (dims, ((), ())), precision=lax.Precision.HI...]
    unnamed x7 -> x2, waiting for transfers between devices: 17.3 us -> 0.03 us
    reduce_scatter x1, waiting for transfers between devices: 37.6 us -> 46.2 us  [on_device(): mine = lax.psum_scatter(sums, 'col', scatter_dimension=0, tiled=True)]
  transfers between devices with their start and end apart: 6 -> 2, of which waited for: 6 -> 2; matrix products, arithmetic and copies ran while one was open for 8% -> 0% of each run, Pallas kernels for 0% -> 0%
where the time goes in v1:
time: 458 us; the launch traced here: 457 us
  waiting for transfers between devices  327 us (71%)
  Pallas kernels  101 us (22%)
  between operations  14.2 us (3%)
  matrix products  6.48 us (1%)
    psum x1, waiting for transfers between devices, on_device(): mine = lax.psum(mine, 'row')  281 us
    pallas_call x1, Pallas kernels, panel_stage(): pl.pallas_call(panel_kernel, out_shape=(jax.ShapeDtypeStruct((80, 512), F...  101 us
    reduce_scatter x1, waiting for transfers between devices, on_device(): mine = lax.psum_scatter(sums, 'col', scatter_dimension=0, tiled=True)  46.2 us
  transfers between devices with their start and end apart: 2, of which 2 were waited for; matrix products, arithmetic and copies ran while one was open for 0% of the time, Pallas kernels for 0%

profile of v1, /device:TPU:1, one launch (start us, length us, event | category | flops | bytes accessed | tf_op | source)
XLA Modules:
  0.0 456.8 jit_solution(1848259987029433086)
XLA Ops:
  7.2 0.0 reduce-scatter.2.cloned.1.call-start
  7.2 101.0 %panels.1 = (f32[80,512]{1,0:T(8,128)}, f32[80,512]{1,0:T(8,128)}, f32[4,80,256]{2,1,0:T(8,128)}) custom-call(f32[640,2560]{1,0:T(8,128)} %k_hbm.1, f32[16,2560]{1,0:T(8,128)} %bitcast.57, f32[16,2560]{1,0:T(8,128)} %bitcast.58, f32[512,512]{1,0:T(8,128)} %coupling.1, s32[160]{0:T(256)} %present_one.1, s32[160]{0:T(256)} %present_two.1), custom_call_target="tpu_custom_call" | custom-call | tf_op jit(solution)/shard_map/panels/pallas_call | solution.py:282
  108.2 0.0 copy-start.2
  108.2 0.0 copy-start.3
  108.2 1.2 reshape.19
  109.4 0.2 copy.35
  109.6 1.5 convolution_bitcast_fusion.1
  111.2 0.0 copy-done.2
  111.2 0.6 convolution_bitcast_fusion
  111.8 0.0 copy-done.3
  111.8 0.6 convolution_bitcast_fusion.2
  112.5 1.9 pad_maximum_fusion
  114.4 0.0 copy-start.1
  114.4 0.0 copy-start
  114.4 0.0 reduce-scatter.2.cloned.1.call-update
  114.4 0.0 all-reduce.2.cloned.1.call-start
  114.5 46.2 %reduce-scatter.2.cloned.1.call-done = f32[64,3,512]{2,0,1:T(8,128)} async-done(((f32[512,3,512]{2,0,1:T(8,128)}), f32[64,3,512]{2,0,1:T(8,128)}) %reduce-scatter.2.cloned.1.call-update) | async-done | bytes 393232 | tf_op jit(solution)/shard_map/reduce_scatter | solution.py:328
  160.7 0.0 all-reduce.2.cloned.1.call-update
  160.8 0.0 copy-done.1
  160.8 1.2 constant_dynamic-slice_fusion
  161.9 0.1 copy.19
  162.1 0.1 copy.18
  162.2 281.1 %all-reduce.2.cloned.1.call-done = f32[64,3,512]{2,0,1:T(8,128)} async-done(((f32[64,3,512]{2,0,1:T(8,128)}), f32[64,3,512]{2,0,1:T(8,128)}) %all-reduce.2.cloned.1.call-update) | async-done | bytes 393232 | tf_op jit(solution)/shard_map/psum | solution.py:329
  443.3 0.0 copy-done
  443.3 1.7 convolution_subtract_fusion
  445.0 0.0 copy-start.4
  445.0 1.6 fusion.10
  446.6 2.0 fusion
  448.6 0.7 copy.39
  449.3 0.7 copy.40
  450.0 0.0 copy-done.4
  (1 shorter events, 0.0 us)
Async XLA Ops:
  7.2 153.6 %reduce-scatter.2.cloned.1.call-start = ((), (), s32[]{:S(2)}) async-start(), calls=%async_computation.1 | async-start | bytes 3538944 | tf_op jit(solution)/shard_map/reduce_scatter | solution.py:328
  108.2 3.0 copy-start.2
  108.2 3.6 copy-start.3
  114.4 46.4 %copy-start.1 = (f32[512,512]{1,0:T(8,128)S(1)}, f32[512,512]{1,0:T(8,128)}, u32[]{:S(2)}) copy-start(f32[512,512]{1,0:T(8,128)} %param.12) | copy-start | bytes 3145732
  114.4 328.9 %copy-start = (f32[512,512]{1,0:T(8,128)S(1)}, f32[512,512]{1,0:T(8,128)}, u32[]{:S(2)}) copy-start(f32[512,512]{1,0:T(8,128)} %coupling.1) | copy-start | bytes 3145732
  114.4 328.8 %all-reduce.2.cloned.1.call-start = ((), (), s32[]{:S(2)}) async-start(), calls=%async_computation.2 | async-start | bytes 786432 | tf_op jit(solution)/shard_map/psum | solution.py:329
  445.0 5.0 %copy-start.4 = (f32[64,512]{1,0:T(8,128)}, f32[64,512]{1,0:T(8,128)S(1)}, u32[]{:S(2)}) copy-start(f32[64,512]{1,0:T(8,128)S(1)} %convolution_subtract_fusion) | copy-start | bytes 393220
Sparse Core Ops, SparseCore 0:
  114.6 46.1 reduce-scatter.1
  163.4 279.8 all-reduce.1

commit v2 on v1

--- a/solution.py
+++ b/solution.py
@@ -45,11 +45,13 @@
             copy.wait_send()
 
 
-def panel_kernel(
-    k_hbm, one_hbm, two_hbm, coupling, present_one, present_two,
-    x1_out, x2_out, p80_out,
-    k_f32, k_hi, k_lo, panels, mask, y, from_x, half_out, half_in, own, turned, y_two,
-    local_sem, send_sem, recv_sem, x_sem, z_sem, p_send, p_recv,
+def update_kernel(
+    k_hbm, one_hbm, two_hbm, coupling, diag_one, diag_two, present_one, present_two,
+    x1_out, x2_out, first_out, cross_out, second_out,
+    k_f32, k_hi, k_lo, panels, mask, y, y_first, y_second, half_out, half_in, own, turned, y_two,
+    pieces, mate_pieces, blocks, mate_blocks, slices, c_split, sums, s_first, s_second, rest, r_first, r_second,
+    z_pair, z_in, over_g, g_in, gathered,
+    local_sem, send_sem, recv_sem, x_sem, z_sem, p_send, p_recv, mate_sem, sum_sem, rest_sem, tail_sem, end_sem,
 ):
     row = lax.axis_index("row")
     col = lax.axis_index("col")
@@ -62,7 +64,8 @@
     y_up, y_down = at(g0, y0 + 1, k0), at(g0, y0 + 3, k0)
     g_up, g_down = at(g0 + 1, y0, k0), at(g0 + 3, y0, k0)
     sibling = at(g0, y0, 1 - k0)
-    x_mate = [(row, z0 * 4 + (x0 + d) % 4) for d in (1, 2, 3)]
+    x_up, x_down = (row, z0 * 4 + (x0 + 1) % 4), (row, z0 * 4 + (x0 + 3) % 4)
+    y_far, g_far = at(g0, y0 + 2, k0), at(g0 + 2, y0, k0)
     z_mate = (row, (1 - z0) * 4 + x0)
     p_target = (col * 4 + row // 8, row % 8)
     p_source = ((row % 4) * 8 + col, row // 4)
@@ -78,7 +81,7 @@
         copy.start()
 
     barrier = pltpu.get_barrier_semaphore()
-    for device in (y_up, y_down, g_up, g_down, sibling, *x_mate, z_mate):
+    for device in (y_up, y_down, y_far, g_up, g_down, g_far, sibling, x_up, x_down, z_mate):
         pl.semaphore_signal(barrier, inc=1, device_id=device, device_id_type=MESH)
 
     @pl.when(jnp.logical_not(stays))
@@ -86,11 +89,35 @@
         pl.semaphore_signal(barrier, inc=1, device_id=p_target, device_id_type=MESH)
         pl.semaphore_signal(barrier, inc=1, device_id=p_source, device_id_type=MESH)
 
-    pl.semaphore_wait(barrier, jnp.where(stays, 9, 11))
+    pl.semaphore_wait(barrier, jnp.where(stays, 10, 12))
     for copy in firsts:
         copy.wait()
 
     send = Sends(send_sem)
+
+    def landed(ref, sem):
+        pltpu.make_async_remote_copy(
+            src_ref=ref, dst_ref=ref, send_sem=send_sem.at[0], recv_sem=sem, device_id=sibling, device_id_type=MESH
+        ).wait_recv()
+
+    def ring_start(src, me, up, down, first, second, sem):
+        send(src((me + 2) % 4, 0), first.at[0], sem.at[0], up)
+        send(src((me + 2) % 4, 1), first.at[1], sem.at[1], down)
+        send(src((me + 1) % 4, 1), second.at[0, 1], sem.at[3], up)
+        send(src((me + 3) % 4, 0), second.at[1, 0], sem.at[4], down)
+
+    def ring_middle(src, me, up, down, first, second, sem):
+        landed(first.at[0], sem.at[0])
+        src((me + 1) % 4, 0)[...] += first[0]
+        send(src((me + 1) % 4, 0), second.at[0, 0], sem.at[2], up)
+        landed(first.at[1], sem.at[1])
+        src((me + 3) % 4, 1)[...] += first[1]
+        send(src((me + 3) % 4, 1), second.at[1, 1], sem.at[5], down)
+
+    def ring_wait(second, sem):
+        for a in (0, 1):
+            for b in (0, 1):
+                landed(second.at[a, b], sem.at[2 + 2 * a + b])
 
     def part(g, p, yy, k):
         return panels.at[g % 4, p, yy % 4, k]
@@ -101,10 +128,7 @@
 
     def arrive(g, p, yy, k):
         ref = part(g, p, yy, k)
-        pltpu.make_async_remote_copy(
-            src_ref=ref, dst_ref=ref, send_sem=send_sem.at[0], recv_sem=recv_sem.at[g % 4, p, yy % 4, k],
-            device_id=sibling, device_id_type=MESH,
-        ).wait_recv()
+        landed(ref, recv_sem.at[g % 4, p, yy % 4, k])
 
     def spread_y(g):
         for p in (0, 1):
@@ -130,6 +154,9 @@
             arrive(g, p, y0 + 2, k0)
             push(g, p, y0 + 2, k0, sibling)
 
+    def x_ring(t):
+        return (lambda x, z: y.at[t, z, x]), x0, x_up, x_down, y_first.at[t], y_second.at[t], x_sem.at[t]
+
     def compute(t, g):
         for yy in range(4):
             for p in (0, 1):
@@ -158,8 +185,7 @@
             return carry
 
         lax.fori_loop(0, 2560 // KSTEP, step, 0)
-        for d in (1, 2, 3):
-            send(y.at[t, :, (x0 + d) % 4], from_x.at[t, d - 1], x_sem.at[t, d - 1], x_mate[d - 1])
+        ring_start(*x_ring(t))
         start = jnp.minimum((row * 80) // BLK, 2560 // BLK - 2) * BLK
         lanes = pl.ds(pl.multiple_of(start, BLK), 256)
         window = panels[group, :, :, :, :, lanes].reshape(2, 16, 8, 256)
@@ -169,39 +195,32 @@
 
         @pl.when(stays)
         def _():
-            copy = pltpu.make_async_copy(piece, p80_out.at[group], local_sem.at[3])
+            copy = pltpu.make_async_copy(piece, pieces.at[group], local_sem.at[3])
             copy.start()
             copy.wait()
 
         @pl.when(jnp.logical_not(stays))
         def _():
             pltpu.make_async_remote_copy(
-                src_ref=piece, dst_ref=p80_out.at[group], send_sem=p_send.at[t], recv_sem=p_recv.at[group],
+                src_ref=piece, dst_ref=pieces.at[group], send_sem=p_send.at[t], recv_sem=p_recv.at[group],
                 device_id=p_target, device_id_type=MESH,
             ).start()
 
     def reduce_x(t):
-        for d in range(3):
-            pltpu.make_async_remote_copy(
-                src_ref=from_x.at[t, d], dst_ref=from_x.at[t, d], send_sem=send_sem.at[0], recv_sem=x_sem.at[t, d],
-                device_id=sibling, device_id_type=MESH,
-            ).wait_recv()
+        ring_wait(y_second.at[t], x_sem.at[t])
 
         def total(z):
-            return y[t, z, x0] + from_x[t, 0, z] + from_x[t, 1, z] + from_x[t, 2, z]
+            return y[t, z, x0] + y_second[t, 0, z] + y_second[t, 1, z]
 
         half_out[t] = total(1 - z0)
         send(half_out.at[t], half_in.at[t], z_sem.at[t], z_mate)
         own[t] = total(z0)
 
     def finish_y(t, g):
-        pltpu.make_async_remote_copy(
-            src_ref=half_in.at[t], dst_ref=half_in.at[t], send_sem=send_sem.at[0], recv_sem=z_sem.at[t],
-            device_id=sibling, device_id_type=MESH,
-        ).wait_recv()
+        landed(half_in.at[t], z_sem.at[t])
         done = own[t] + half_in[t]
         lanes = pl.ds(pl.multiple_of((g % 4) * BLK, BLK), BLK)
-        x1_out[:, lanes] = -done[:, :BLK]
+        blocks[0, :, lanes] = -done[:, :BLK]
         y_two[:, lanes] = done[:, BLK:]
 
     order = (g0, g0 + 1, g0 + 3, g0 + 2)
@@ -227,6 +246,13 @@
         return carry
 
     lax.fori_loop(0, 20, split_rows, 0)
+    hi, lo = split(coupling[...])
+    c_split[0] = hi
+    c_split[1] = lo
+    pair = pl.ds(pl.multiple_of((col // 2) * BLK, BLK), BLK)
+    for i, ref in enumerate((coupling, diag_one, diag_two)):
+        slices[i] = ref[:, pair].T
+    mine = pl.ds(pl.multiple_of((col % 2) * 64, 64), 64)
 
     relay_y(order[0])
     arrive(g0 + 3, 0, y0, k0)
@@ -240,6 +266,7 @@
     relay_y(order[1])
     arrive(g0 + 3, 1, y0, k0)
     spread_y(order[2])
+    ring_middle(*x_ring(0))
     end_y(order[1])
     compute(1, order[1])
     reduce_x(0)
@@ -247,47 +274,147 @@
     arrive(g0 + 2, 0, y0, k0)
     arrive(g0 + 2, 1, y0, k0)
     spread_y(order[3])
+    ring_middle(*x_ring(1))
     end_y(order[2])
     compute(2, order[2])
     reduce_x(1)
     finish_y(0, order[0])
     relay_y(order[3])
+    ring_middle(*x_ring(2))
+    diag_coupled = dot3(slices[0, mine, :], diag_one[...], ((1,), (1,)))
     end_y(order[3])
     compute(3, order[3])
     reduce_x(2)
     finish_y(1, order[1])
+    ring_middle(*x_ring(3))
+    finish_y(2, order[2])
     reduce_x(3)
-    finish_y(2, order[2])
     finish_y(3, order[3])
-    x2_out[...] = -(y_two[...] + dot3(x1_out[...], coupling[...], ((1,), (0,))))
-
-    send.finish()
+
+    def times_coupling(left):
+        lh, ll = split(left)
+        g = functools.partial(jnp.dot, preferred_element_type=F32)
+        return g(lh, c_split[0]) + (g(lh, c_split[1]) + g(ll, c_split[0]))
+
+    blocks[1] = -(y_two[...] + times_coupling(blocks[0]))
+    send(blocks, mate_blocks, mate_sem.at[0], sibling)
 
     @pl.when(jnp.logical_not(stays))
     def _():
         for t in range(4):
             copy = pltpu.make_async_remote_copy(
-                src_ref=turned.at[t, pl.ds(0, 80)], dst_ref=p80_out.at[t], send_sem=p_send.at[t],
+                src_ref=turned.at[t, pl.ds(0, 80)], dst_ref=pieces.at[t], send_sem=p_send.at[t],
                 recv_sem=p_recv.at[t], device_id=p_target, device_id_type=MESH,
             )
             copy.wait_send()
             copy.wait_recv()
 
-
-def panel_stage(known_inverse, one, two, coupling, present_one, present_two):
+    send(pieces.at[pl.ds(2 * (1 - k0), 2)], mate_pieces, mate_sem.at[1], sibling)
+    x1_out[...] = blocks[0]
+    x2_out[...] = blocks[1]
+    landed(mate_pieces, mate_sem.at[1])
+    landed(mate_blocks, mate_sem.at[0])
+
+    for side in (0, 1):
+        lanes = slice(side * BLK, side * BLK + BLK)
+        right = jnp.concatenate(
+            [
+                jnp.concatenate([pieces[2 * k0], pieces[2 * k0 + 1]], axis=1),
+                jnp.concatenate([mate_pieces[0], mate_pieces[1]], axis=1),
+            ],
+            axis=0,
+        )
+        if side == 0:
+            one = jnp.concatenate([right[:, 0:128], right[:, 256:384]], axis=1)
+            two = jnp.concatenate([right[:, 128:256], right[:, 384:512]], axis=1)
+            left = [jnp.concatenate([blocks[i], mate_blocks[i]], axis=0) for i in (0, 1)]
+            products = [
+                dot3(left[i], p, ((0,), (0,))).reshape(2, 4, 4, 16, 256) for i, p in ((0, one), (1, one), (1, two))
+            ]
+        for j, value in enumerate(products):
+            for z in (0, 1):
+                for w in range(4):
+                    if side == 0:
+                        sums[0, w, z, :, j] = value[z, w, :, :, :BLK]
+                    else:
+                        sums[1, w, z, :, j] = value[z, :, w, :, BLK:]
+
+    ring_x, ring_y = (x0, x_up, x_down), (y0, y_up, y_down)
+    whole = [
+        ((lambda w, z, side=side: sums.at[side, w, z]), *ring, s_first.at[side], s_second.at[side], sum_sem.at[side])
+        for side, ring in ((0, ring_x), (1, ring_y))
+    ]
+    part_of = [
+        ((lambda w, z, side=side: rest.at[side, w, z]), *ring, r_first.at[side], r_second.at[side], rest_sem.at[side])
+        for side, ring in ((0, ring_y), (1, ring_x))
+    ]
+    for side in (0, 1):
+        ring_start(*whole[side])
+    for side in (0, 1):
+        ring_middle(*whole[side])
+    for side in (0, 1):
+        ring_wait(s_second.at[side], sum_sem.at[side])
+        me = (x0, y0)[side]
+        for z in (0, 1):
+            rest[side, :, z] = sums[side, me, z] + s_second[side, 0, z] + s_second[side, 1, z]
+        ring_start(*part_of[side])
+    for side in (0, 1):
+        ring_middle(*part_of[side])
+    for side in (0, 1):
+        ring_wait(r_second.at[side], rest_sem.at[side])
+        me = (y0, x0)[side]
+        for z in (0, 1):
+            z_pair[z, side] = rest[side, me, z] + r_second[side, 0, z] + r_second[side, 1, z]
+    send(z_pair.at[1 - z0], z_in, tail_sem.at[0], z_mate)
+    landed(z_in, tail_sem.at[0])
+    over_g[...] = z_pair[z0] + z_in[...]
+    for d, device in enumerate((g_up, g_down, g_far)):
+        send(over_g, g_in.at[d], tail_sem.at[1 + d], device)
+    for d in range(3):
+        landed(g_in.at[d], tail_sem.at[1 + d])
+    even = over_g[...] + g_in[2]
+    odd = g_in[0] + g_in[1]
+    gathered[k0, y0] = even + odd
+    mine_ref = gathered.at[k0, y0]
+    for device in (y_up, y_down, y_far, sibling):
+        send(mine_ref, mine_ref, end_sem.at[k0, y0], device)
+    for d in (1, 3, 2):
+        ref = gathered.at[k0, (y0 + d) % 4]
+        landed(ref, end_sem.at[k0, (y0 + d) % 4])
+        send(ref, ref, end_sem.at[k0, (y0 + d) % 4], sibling)
+    for d in range(4):
+        ref = gathered.at[1 - k0, (y0 + d) % 4]
+        landed(ref, end_sem.at[1 - k0, (y0 + d) % 4])
+
+    def total_of(j):
+        return jnp.concatenate(
+            [
+                jnp.concatenate([gathered[k, w, side, j] for w in range(4)], axis=0)
+                for k in (0, 1)
+                for side in (0, 1)
+            ],
+            axis=1,
+        )
+
+    first_out[...] = slices[1, mine, :] - total_of(0)
+    cross = -total_of(1) - diag_coupled
+    cross_out[...] = cross
+    second_out[...] = slices[2, mine, :] - total_of(2) - times_coupling(cross)
+    send.finish()
+
+
+def update(known_inverse, one, two, coupling, diag_one, diag_two, present_one, present_two):
     vmem = pl.BlockSpec(memory_space=pltpu.VMEM)
     hbm = pl.BlockSpec(memory_space=pl.ANY)
     smem = pl.BlockSpec(memory_space=pltpu.SMEM)
     dma = pltpu.SemaphoreType.DMA
+    tall = jax.ShapeDtypeStruct((80, 512), F32)
+    small = jax.ShapeDtypeStruct((64, 512), F32)
     return pl.pallas_call(
-        panel_kernel,
-        out_shape=(
-            jax.ShapeDtypeStruct((80, 512), F32),
-            jax.ShapeDtypeStruct((80, 512), F32),
-            jax.ShapeDtypeStruct((4, 80, 256), F32),
-        ),
-        in_specs=[hbm, hbm, hbm, vmem, smem, smem],
-        out_specs=(vmem, vmem, vmem),
+        update_kernel,
+        out_shape=(tall, tall, small, small, small),
+        in_specs=[hbm, hbm, hbm, vmem, vmem, vmem, smem, smem],
+        out_specs=(vmem,) * 5,
         scratch_shapes=[
             pltpu.VMEM((640, 2560), F32),
             pltpu.VMEM((640, 2560), BF16),
@@ -295,46 +422,55 @@
             pltpu.VMEM((4, 2, 4, 2, 16, 2560), F32),
             pltpu.VMEM((2, 8, 2560), F32),
             pltpu.VMEM((4, 2, 4, 80, 256), F32),
-            pltpu.VMEM((4, 3, 2, 80, 256), F32),
+            pltpu.VMEM((4, 2, 80, 256), F32),
+            pltpu.VMEM((4, 2, 2, 80, 256), F32),
             pltpu.VMEM((4, 80, 256), F32),
             pltpu.VMEM((4, 80, 256), F32),
             pltpu.VMEM((4, 80, 256), F32),
             pltpu.VMEM((4, 256, 256), F32),
             pltpu.VMEM((80, 512), F32),
+            pltpu.VMEM((4, 80, 256), F32),
+            pltpu.VMEM((2, 80, 256), F32),
+            pltpu.VMEM((2, 80, 512), F32),
+            pltpu.VMEM((2, 80, 512), F32),
+            pltpu.VMEM((3, 128, 512), F32),
+            pltpu.VMEM((2, 512, 512), BF16),
+            pltpu.VMEM((2, 4, 2, 4, 3, 16, 128), F32),
+            pltpu.VMEM((2, 2, 4, 3, 16, 128), F32),
+            pltpu.VMEM((2, 2, 2, 4, 3, 16, 128), F32),
+            pltpu.VMEM((2, 4, 2, 3, 16, 128), F32),
+            pltpu.VMEM((2, 2, 3, 16, 128), F32),
+            pltpu.VMEM((2, 2, 2, 3, 16, 128), F32),
+            pltpu.VMEM((2, 2, 3, 16, 128), F32),
+            pltpu.VMEM((2, 3, 16, 128), F32),
+            pltpu.VMEM((2, 3, 16, 128), F32),
+            pltpu.VMEM((3, 2, 3, 16, 128), F32),
+            pltpu.VMEM((2, 4, 2, 3, 16, 128), F32),
             dma((4,)),
-            dma((82,)),
+            dma((140,)),
             dma((4, 2, 4, 2)),
-            dma((4, 3)),
+            dma((4, 6)),
             dma((4,)),
             dma((4,)),
             dma((4,)),
+            dma((2,)),
+            dma((2, 6)),
+            dma((2, 6)),
+            dma((4,)),
+            dma((2, 4)),
         ],
         compiler_params=pltpu.CompilerParams(
             collective_id=0, has_side_effects=True, vmem_limit_bytes=56 * 2**20
         ),
-        name="panels",
-    )(known_inverse, one, two, coupling, present_one, present_two)
-
-
-def dot_high(left, right, dims):
-    return lax.dot_general(left, right, (dims, ((), ())), precision=lax.Precision.HIGH, preferred_element_type=F32)
+        name="update",
+    )(known_inverse, one, two, coupling, diag_one, diag_two, present_one, present_two)
 
 
 def on_device(known_inverse, first_panel, second_panel, coupling, first_diag, second_diag, first_present, second_present):
-    x1, x2, p80 = panel_stage(known_inverse, first_panel.T, second_panel.T, coupling, first_present, second_present)
-    p = p80.reshape(4, 80, 2, 128).transpose(2, 1, 0, 3).reshape(2, 80, 512)
-    rows = ((0,), (0,))
-    sums = jnp.stack([dot_high(x1, p[0], rows), dot_high(x2, p[0], rows), dot_high(x2, p[1], rows)], axis=1)
-    mine = lax.psum_scatter(sums, "col", scatter_dimension=0, tiled=True)
-    mine = lax.psum(mine, "row")
-    start = lax.axis_index("col") * 64
-    diag_one = lax.dynamic_slice_in_dim(first_diag, start, 64, 1)
-    diag_two = lax.dynamic_slice_in_dim(second_diag, start, 64, 1)
-    coupling_part = lax.dynamic_slice_in_dim(coupling, start, 64, 1)
-    first_out = diag_one - mine[:, 0].T
-    cross = -mine[:, 1].T - dot_high(first_diag, coupling_part, ((1,), (0,)))
-    second_out = diag_two - mine[:, 2].T - dot_high(coupling, cross, ((0,), (0,)))
-    return x1, first_out, x2, cross, second_out
+    x1, x2, first, cross, second = update(
+        known_inverse, first_panel.T, second_panel.T, coupling, first_diag, second_diag, first_present, second_present
+    )
+    return x1, first.T, x2, cross.T, second.T
 
 
 def solution(mesh):

time: 458 us -> 143 us (0.31)
  waiting for transfers between devices: 327 us -> 0 us
  Pallas kernels: 101 us -> 134 us
  between operations: 14.2 us -> 0.64 us
  matrix products: 6.48 us -> 0 us
    psum x1 -> x0, waiting for transfers between devices: 281 us -> none  [on_device(): mine = lax.psum(mine, 'row')]
    reduce_scatter x1 -> x0, waiting for transfers between devices: 46.2 us -> none  [on_device(): mine = lax.psum_scatter(sums, 'col', scatter_dimension=0, tiled=True)]
    pallas_call x1, Pallas kernels: 101 us -> 134 us  [update(): pl.pallas_call(update_kernel, out_shape=(tall, tall, small, small, small)...]
    dot_general x5 -> x0, matrix products: 6.48 us -> none  [dot_high(): lax.dot_general(left, right, (dims, ((), ())), precision=lax.Precision.HI...]
    unnamed x14 -> x5, local copies, waits for them, and re-layouts: 1.58 us -> 7.89 us
  transfers between devices with their start and end apart: 2 -> 0, of which waited for: 2 -> 0; matrix products, arithmetic and copies ran while one was open for 0% -> 0% of each run, Pallas kernels for 0% -> 0%
where the time goes in v2:
time: 143 us; the launch traced here: 142 us
  Pallas kernels  134 us (94%)
  local copies, waits for them, and re-layouts  7.89 us (6%)
    pallas_call x1, Pallas kernels, update(): pl.pallas_call(update_kernel, out_shape=(tall, tall, small, small, small)...  134 us
    unnamed x5, local copies, waits for them, and re-layouts  7.89 us

profile of v2, /device:TPU:1, one launch (start us, length us, event | category | flops | bytes accessed | tf_op | source)
XLA Modules:
  0.0 142.4 jit_solution(16159590646508352655)
XLA Ops:
  0.6 133.9 %update.1 = (f32[80,512]{1,0:T(8,128)}, f32[80,512]{1,0:T(8,128)}, f32[64,512]{1,0:T(8,128)}, f32[64,512]{1,0:T(8,128)}, f32[64,512]{1,0:T(8,128)}) custom-call(f32[640,2560]{1,0:T(8,128)} %k_hbm.1, f32[16,2560]{1,0:T(8,128)} %bitcast.5, f32[16,2560]{1,0:T(8,128)} %bitcast.6, f32[512,512]{1,0:T(8,128)} %coupling.1, f32[512,512]{1,0:T(8,128)} %diag_one.1, ...), custom_call_target="tpu_custom_call" | custom-call | tf_op jit(solution)/shard_map/update/pallas_call | solution.py:413
  134.5 1.6 %copy.18 = f32[80,512]{1,0:T(8,128)} copy(f32[80,512]{1,0:T(8,128)} %get-tuple-element.20) | data formatting | bytes 327680
  136.1 1.6 %copy.19 = f32[512,64]{0,1:T(8,128)} copy(f32[512,64]{0,1:T(8,128)} %bitcast.9) | data formatting | bytes 262144
  137.7 1.6 %copy.20 = f32[80,512]{1,0:T(8,128)} copy(f32[80,512]{1,0:T(8,128)} %get-tuple-element.22) | data formatting | bytes 327680
  139.3 1.6 %copy.21 = f32[512,64]{0,1:T(8,128)} copy(f32[512,64]{0,1:T(8,128)} %bitcast.8) | data formatting | bytes 262144
  140.8 1.6 %copy.22 = f32[512,64]{0,1:T(8,128)} copy(f32[512,64]{0,1:T(8,128)} %bitcast.7) | data formatting | bytes 262144

commit v3 on v2

--- a/solution.py
+++ b/solution.py
@@ -67,9 +67,19 @@
     x_up, x_down = (row, z0 * 4 + (x0 + 1) % 4), (row, z0 * 4 + (x0 + 3) % 4)
     y_far, g_far = at(g0, y0 + 2, k0), at(g0 + 2, y0, k0)
     z_mate = (row, (1 - z0) * 4 + x0)
-    p_target = (col * 4 + row // 8, row % 8)
-    p_source = ((row % 4) * 8 + col, row // 4)
-    stays = jnp.logical_and(p_target[0] == row, p_target[1] == col)
+    hands_out = g0 == col // 2
+    level = (y0 // 2) == (col % 2)
+    y_to = jnp.where(level, y0, 3 - y0)
+    to_row = g0 * 8 + y_to * 2 + k0
+    x_first = x0 + jnp.where(level, 0, 2)
+
+    def to_col(i):
+        return (i // 2) * 4 + (x_first + i % 2) % 4
+
+    giver_col = row // 4
+    y_from = jnp.where((x0 - giver_col % 4 + 4) % 4 < 2, y0, 3 - y0)
+    giver = (g0 * 8 + y_from * 2 + k0, giver_col)
+    stays = jnp.logical_and(giver[0] == row, giver_col == col)
 
     k_copy = pltpu.make_async_copy(k_hbm, k_f32, local_sem.at[0])
     k_copy.start()
@@ -84,12 +94,19 @@
     for device in (y_up, y_down, y_far, g_up, g_down, g_far, sibling, x_up, x_down, z_mate):
         pl.semaphore_signal(barrier, inc=1, device_id=device, device_id_type=MESH)
 
+    @pl.when(hands_out)
+    def _():
+        for i in range(4):
+            @pl.when(jnp.logical_not(jnp.logical_and(to_row == row, to_col(i) == col)))
+            def _():
+                pl.semaphore_signal(barrier, inc=1, device_id=(to_row, to_col(i)), device_id_type=MESH)
+
     @pl.when(jnp.logical_not(stays))
     def _():
-        pl.semaphore_signal(barrier, inc=1, device_id=p_target, device_id_type=MESH)
-        pl.semaphore_signal(barrier, inc=1, device_id=p_source, device_id_type=MESH)
-
-    pl.semaphore_wait(barrier, jnp.where(stays, 10, 12))
+        pl.semaphore_signal(barrier, inc=1, device_id=giver, device_id_type=MESH)
+
+    extra = jnp.where(hands_out, 4, 0) + jnp.where(stays, -1, 1)
+    pl.semaphore_wait(barrier, 10 + extra)
     for copy in firsts:
         copy.wait()
 
@@ -186,25 +203,34 @@
 
         lax.fori_loop(0, 2560 // KSTEP, step, 0)
         ring_start(*x_ring(t))
-        start = jnp.minimum((row * 80) // BLK, 2560 // BLK - 2) * BLK
-        lanes = pl.ds(pl.multiple_of(start, BLK), 256)
-        window = panels[group, :, :, :, :, lanes].reshape(2, 16, 8, 256)
-        window = (window * mask[:, :, lanes][:, None]).reshape(256, 256)
-        turned[t] = window.T
-        piece = turned.at[t, pl.ds(pl.multiple_of(row * 80 - start, 8), 80)]
-
-        @pl.when(stays)
+        def hand(i):
+            target = to_col(i)
+            first_row = (((y_to % 2) * 2 + k0) * 8 + target) * 80
+            start = jnp.minimum(first_row // BLK, 2560 // BLK - 2) * BLK
+            lanes = pl.ds(pl.multiple_of(start, BLK), 256)
+            window = panels[group, :, :, :, :, lanes].reshape(2, 16, 8, 256)
+            window = (window * mask[:, :, lanes][:, None]).reshape(256, 256)
+            turned[t, i] = window.T
+            piece = turned.at[t, i, pl.ds(pl.multiple_of(first_row - start, 8), 80)]
+            same = jnp.logical_and(to_row == row, target == col)
+
+            @pl.when(same)
+            def _():
+                copy = pltpu.make_async_copy(piece, pieces.at[group], local_sem.at[3])
+                copy.start()
+                copy.wait()
+
+            @pl.when(jnp.logical_not(same))
+            def _():
+                pltpu.make_async_remote_copy(
+                    src_ref=piece, dst_ref=pieces.at[group], send_sem=p_send.at[t, i], recv_sem=p_recv.at[group],
+                    device_id=(to_row, target), device_id_type=MESH,
+                ).start()
+
+        @pl.when(hands_out)
         def _():
-            copy = pltpu.make_async_copy(piece, pieces.at[group], local_sem.at[3])
-            copy.start()
-            copy.wait()
-
-        @pl.when(jnp.logical_not(stays))
-        def _():
-            pltpu.make_async_remote_copy(
-                src_ref=piece, dst_ref=pieces.at[group], send_sem=p_send.at[t], recv_sem=p_recv.at[group],
-                device_id=p_target, device_id_type=MESH,
-            ).start()
+            for i in range(4):
+                hand(i)
 
     def reduce_x(t):
         ring_wait(y_second.at[t], x_sem.at[t])
@@ -301,13 +327,8 @@
 
     @pl.when(jnp.logical_not(stays))
     def _():
-        for t in range(4):
-            copy = pltpu.make_async_remote_copy(
-                src_ref=turned.at[t, pl.ds(0, 80)], dst_ref=pieces.at[t], send_sem=p_send.at[t],
-                recv_sem=p_recv.at[t], device_id=p_target, device_id_type=MESH,
-            )
-            copy.wait_send()
-            copy.wait_recv()
+        for g in range(4):
+            landed(pieces.at[g], p_recv.at[g])
 
     send(pieces.at[pl.ds(2 * (1 - k0), 2)], mate_pieces, mate_sem.at[1], sibling)
     x1_out[...] = blocks[0]
@@ -402,6 +423,17 @@
     second_out[...] = slices[2, mine, :] - total_of(2) - times_coupling(cross)
     send.finish()
 
+    @pl.when(hands_out)
+    def _():
+        for i in range(4):
+            @pl.when(jnp.logical_not(jnp.logical_and(to_row == row, to_col(i) == col)))
+            def _():
+                for t in range(4):
+                    pltpu.make_async_remote_copy(
+                        src_ref=turned.at[t, i, pl.ds(0, 80)], dst_ref=pieces.at[t], send_sem=p_send.at[t, i],
+                        recv_sem=p_recv.at[t], device_id=giver, device_id_type=MESH,
+                    ).wait_send()
+
 
 def update(known_inverse, one, two, coupling, diag_one, diag_two, present_one, present_two):
     vmem = pl.BlockSpec(memory_space=pltpu.VMEM)
@@ -427,7 +459,7 @@
             pltpu.VMEM((4, 80, 256), F32),
             pltpu.VMEM((4, 80, 256), F32),
             pltpu.VMEM((4, 80, 256), F32),
-            pltpu.VMEM((4, 256, 256), F32),
+            pltpu.VMEM((4, 4, 256, 256), F32),
             pltpu.VMEM((80, 512), F32),
             pltpu.VMEM((4, 80, 256), F32),
             pltpu.VMEM((2, 80, 256), F32),
@@ -451,7 +483,7 @@
             dma((4, 2, 4, 2)),
             dma((4, 6)),
             dma((4,)),
-            dma((4,)),
+            dma((4, 4)),
             dma((4,)),
             dma((2,)),
             dma((2, 6)),
@@ -466,9 +498,27 @@
     )(known_inverse, one, two, coupling, diag_one, diag_two, present_one, present_two)
 
 
+def emit_kernel(*refs):
+    for source, target in zip(refs[:5], refs[5:]):
+        target[...] = source[...]
+
+
+def emit(*arrays):
+    vmem = pl.BlockSpec(memory_space=pltpu.VMEM)
+    return pl.pallas_call(
+        emit_kernel,
+        out_shape=tuple(jax.ShapeDtypeStruct(a.shape, a.dtype) for a in arrays),
+        in_specs=[vmem] * 5,
+        out_specs=(vmem,) * 5,
+        name="emit",
+    )(*arrays)
+
+
 def on_device(known_inverse, first_panel, second_panel, coupling, first_diag, second_diag, first_present, second_present):
-    x1, x2, first, cross, second = update(
-        known_inverse, first_panel.T, second_panel.T, coupling, first_diag, second_diag, first_present, second_present
+    x1, x2, first, cross, second = emit(
+        *update(
+            known_inverse, first_panel.T, second_panel.T, coupling, first_diag, second_diag, first_present, second_present
+        )
     )
     return x1, first.T, x2, cross.T, second.T
 

time: 143 us -> 131 us (0.916)
  local copies, waits for them, and re-layouts: 7.89 us -> 0 us
  Pallas kernels: 134 us -> 131 us
    unnamed x5 -> x0, local copies, waits for them, and re-layouts: 7.89 us -> none
    pallas_call x1, Pallas kernels: 134 us -> 128 us  [update(): pl.pallas_call(update_kernel, out_shape=(tall, tall, small, small, small)...]
    pallas_call x0 -> x1, Pallas kernels: none -> 2.06 us  [emit(): pl.pallas_call(emit_kernel, out_shape=tuple((jax.ShapeDtypeStruct(a.shape...]
where the time goes in v3:
time: 131 us
  Pallas kernels  131 us (100%)
    pallas_call x1, Pallas kernels, update(): pl.pallas_call(update_kernel, out_shape=(tall, tall, small, small, small)...  128 us

profile of v3, /device:TPU:1, one launch (start us, length us, event | category | flops | bytes accessed | tf_op | source)
XLA Modules:
  0.0 131.1 jit_solution(14931220420576863121)
XLA Ops:
  0.6 128.4 %update.1 = (f32[80,512]{1,0:T(8,128)}, f32[80,512]{1,0:T(8,128)}, f32[64,512]{1,0:T(8,128)}, f32[64,512]{1,0:T(8,128)}, f32[64,512]{1,0:T(8,128)}) custom-call(f32[640,2560]{1,0:T(8,128)} %k_hbm.1, f32[16,2560]{1,0:T(8,128)} %bitcast.5, f32[16,2560]{1,0:T(8,128)} %bitcast.6, f32[512,512]{1,0:T(8,128)} %coupling.1, f32[512,512]{1,0:T(8,128)} %diag_one.1, ...), custom_call_target="tpu_custom_call" | custom-call | tf_op jit(solution)/shard_map/update/pallas_call | solution.py:445
  129.1 2.1 %emit.1 = (f32[80,512]{1,0:T(8,128)}, f32[80,512]{1,0:T(8,128)}, f32[64,512]{1,0:T(8,128)}, f32[64,512]{1,0:T(8,128)}, f32[64,512]{1,0:T(8,128)}) custom-call(f32[80,512]{1,0:T(8,128)} %get-tuple-element.15.refs_0_, f32[80,512]{1,0:T(8,128)} %get-tuple-element.16.refs_1_, f32[64,512]{1,0:T(8,128)} %get-tuple-element.17.refs_2_, ...), custom_call_target="tpu_custom_call" | custom-call | tf_op jit(solution)/shard_map/emit/pallas_call | solution.py:508

commit v4 on v3

--- a/solution.py
+++ b/solution.py
@@ -46,10 +46,11 @@
 
 
 def update_kernel(
-    k_hbm, one_hbm, two_hbm, coupling, diag_one, diag_two, present_one, present_two,
+    k_hbm, one_hbm, two_hbm, c_hbm, d_one_hbm, d_two_hbm, present_one, present_two,
     x1_out, x2_out, first_out, cross_out, second_out,
+    coupling, diag_one, diag_two,
     k_f32, k_hi, k_lo, panels, mask, y, y_first, y_second, half_out, half_in, own, turned, y_two,
-    pieces, mate_pieces, blocks, mate_blocks, slices, c_split, sums, s_first, s_second, rest, r_first, r_second,
+    pieces, mate_pieces, blocks, mate_blocks, slices, c_split, sums_a, a_first, a_second, sums_b, b_first, b_second, rest, r_first, r_second,
     z_pair, z_in, over_g, g_in, gathered,
     local_sem, send_sem, recv_sem, x_sem, z_sem, p_send, p_recv, mate_sem, sum_sem, rest_sem, tail_sem, end_sem,
 ):
@@ -82,7 +83,6 @@
     stays = jnp.logical_and(giver[0] == row, giver_col == col)
 
     k_copy = pltpu.make_async_copy(k_hbm, k_f32, local_sem.at[0])
-    k_copy.start()
     firsts = [
         pltpu.make_async_copy(one_hbm, panels.at[g0, 0, y0, k0], local_sem.at[1]),
         pltpu.make_async_copy(two_hbm, panels.at[g0, 1, y0, k0], local_sem.at[2]),
@@ -109,6 +109,10 @@
     pl.semaphore_wait(barrier, 10 + extra)
     for copy in firsts:
         copy.wait()
+    squares = [
+        pltpu.make_async_copy(source, target, local_sem.at[i])
+        for i, source, target in ((4, c_hbm, coupling), (5, d_one_hbm, diag_one), (6, d_two_hbm, diag_two))
+    ]
 
     send = Sends(send_sem)
 
@@ -227,10 +231,15 @@
                     device_id=(to_row, target), device_id_type=MESH,
                 ).start()
 
-        @pl.when(hands_out)
-        def _():
-            for i in range(4):
-                hand(i)
+        def hand_all():
+            @pl.when(hands_out)
+            def _():
+                for i in range(4):
+                    hand(i)
+
+        if t < 3:
+            hand_all()
+        return hand_all
 
     def reduce_x(t):
         ring_wait(y_second.at[t], x_sem.at[t])
@@ -257,6 +266,9 @@
         push(g0, p, y0, k0, g_up)
         push(g0, 1 - p, y0, k0, g_down)
         push(g0, p, y0, k0, sibling)
+    k_copy.start()
+    for copy in squares:
+        copy.start()
 
     for p, present in ((0, present_one), (1, present_two)):
         for j in range(2560 // BLK):
@@ -272,13 +284,6 @@
         return carry
 
     lax.fori_loop(0, 20, split_rows, 0)
-    hi, lo = split(coupling[...])
-    c_split[0] = hi
-    c_split[1] = lo
-    pair = pl.ds(pl.multiple_of((col // 2) * BLK, BLK), BLK)
-    for i, ref in enumerate((coupling, diag_one, diag_two)):
-        slices[i] = ref[:, pair].T
-    mine = pl.ds(pl.multiple_of((col % 2) * 64, 64), 64)
 
     relay_y(order[0])
     arrive(g0 + 3, 0, y0, k0)
@@ -289,6 +294,15 @@
     arrive(g0 + 1, 0, y0, k0)
     spread_y(order[1])
     compute(0, order[0])
+    for copy in squares:
+        copy.wait()
+    hi, lo = split(coupling[...])
+    c_split[0] = hi
+    c_split[1] = lo
+    pair = pl.ds(pl.multiple_of((col // 2) * BLK, BLK), BLK)
+    for i, ref in enumerate((coupling, diag_one, diag_two)):
+        slices[i] = ref[:, pair].T
+    mine = pl.ds(pl.multiple_of((col % 2) * 64, 64), 64)
     relay_y(order[1])
     arrive(g0 + 3, 1, y0, k0)
     spread_y(order[2])
@@ -309,12 +323,19 @@
     ring_middle(*x_ring(2))
     diag_coupled = dot3(slices[0, mine, :], diag_one[...], ((1,), (1,)))
     end_y(order[3])
-    compute(3, order[3])
+    hand_last = compute(3, order[3])
     reduce_x(2)
     finish_y(1, order[1])
     ring_middle(*x_ring(3))
+    hand_last()
     finish_y(2, order[2])
     reduce_x(3)
+    @pl.when(jnp.logical_not(stays))
+    def _():
+        for g in range(4):
+            landed(pieces.at[g], p_recv.at[g])
+
+    send(pieces.at[pl.ds(2 * (1 - k0), 2)], mate_pieces, mate_sem.at[1], sibling)
     finish_y(3, order[3])
 
     def times_coupling(left):
@@ -322,62 +343,69 @@
         g = functools.partial(jnp.dot, preferred_element_type=F32)
         return g(lh, c_split[0]) + (g(lh, c_split[1]) + g(ll, c_split[0]))
 
+    send(blocks.at[0], mate_blocks.at[0], mate_sem.at[0], sibling)
     blocks[1] = -(y_two[...] + times_coupling(blocks[0]))
-    send(blocks, mate_blocks, mate_sem.at[0], sibling)
-
-    @pl.when(jnp.logical_not(stays))
-    def _():
-        for g in range(4):
-            landed(pieces.at[g], p_recv.at[g])
-
-    send(pieces.at[pl.ds(2 * (1 - k0), 2)], mate_pieces, mate_sem.at[1], sibling)
+    send(blocks.at[1], mate_blocks.at[1], mate_sem.at[2], sibling)
+
     x1_out[...] = blocks[0]
     x2_out[...] = blocks[1]
     landed(mate_pieces, mate_sem.at[1])
-    landed(mate_blocks, mate_sem.at[0])
-
+    landed(mate_blocks.at[0], mate_sem.at[0])
+
+    right = jnp.concatenate(
+        [
+            jnp.concatenate([pieces[2 * k0], pieces[2 * k0 + 1]], axis=1),
+            jnp.concatenate([mate_pieces[0], mate_pieces[1]], axis=1),
+        ],
+        axis=0,
+    )
+    both = jnp.concatenate([right[:, 0:128], right[:, 256:384], right[:, 128:256], right[:, 384:512]], axis=1)
+    both_hi, both_lo = split(both)
+
+    def turned_times(i, width):
+        left = jnp.concatenate([blocks[i].T, mate_blocks[i].T], axis=1)
+        lh, ll = split(left)
+        g = functools.partial(jnp.dot, preferred_element_type=F32)
+        rh, rl = both_hi[:, :width], both_lo[:, :width]
+        return g(lh, rh) + (g(lh, rl) + g(ll, rh))
+
+    def place(sums, j, value):
+        value = value.reshape(2, 4, 4, 16, 256)
+        for z in (0, 1):
+            for w in range(4):
+                sums[0, w, z, :, j] = value[z, w, :, :, :BLK]
+                sums[1, w, z, :, j] = value[z, :, w, :, BLK:]
+
+    ring_x, ring_y = (x0, x_up, x_down), (y0, y_up, y_down)
+    steps = ((sums_a, a_first, a_second), (sums_b, b_first, b_second))
+
+    def whole(i, side):
+        sums, first, second = steps[i]
+        ring = (ring_x, ring_y)[side]
+        return (lambda w, z: sums.at[side, w, z]), *ring, first.at[side], second.at[side], sum_sem.at[i, side]
+
+    place(sums_a, 0, turned_times(0, 256))
     for side in (0, 1):
-        lanes = slice(side * BLK, side * BLK + BLK)
-        right = jnp.concatenate(
-            [
-                jnp.concatenate([pieces[2 * k0], pieces[2 * k0 + 1]], axis=1),
-                jnp.concatenate([mate_pieces[0], mate_pieces[1]], axis=1),
-            ],
-            axis=0,
-        )
-        if side == 0:
-            one = jnp.concatenate([right[:, 0:128], right[:, 256:384]], axis=1)
-            two = jnp.concatenate([right[:, 128:256], right[:, 384:512]], axis=1)
-            left = [jnp.concatenate([blocks[i], mate_blocks[i]], axis=0) for i in (0, 1)]
-            products = [
-                dot3(left[i], p, ((0,), (0,))).reshape(2, 4, 4, 16, 256) for i, p in ((0, one), (1, one), (1, two))
-            ]
-        for j, value in enumerate(products):
-            for z in (0, 1):
-                for w in range(4):
-                    if side == 0:
-                        sums[0, w, z, :, j] = value[z, w, :, :, :BLK]
-                    else:
-                        sums[1, w, z, :, j] = value[z, :, w, :, BLK:]
-
-    ring_x, ring_y = (x0, x_up, x_down), (y0, y_up, y_down)
-    whole = [
-        ((lambda w, z, side=side: sums.at[side, w, z]), *ring, s_first.at[side], s_second.at[side], sum_sem.at[side])
-        for side, ring in ((0, ring_x), (1, ring_y))
-    ]
+        ring_start(*whole(0, side))
+    landed(mate_blocks.at[1], mate_sem.at[2])
+    later = turned_times(1, 512)
+    place(sums_b, 0, later[:, :256])
+    place(sums_b, 1, later[:, 256:])
+    for side in (0, 1):
+        ring_start(*whole(1, side))
     part_of = [
         ((lambda w, z, side=side: rest.at[side, w, z]), *ring, r_first.at[side], r_second.at[side], rest_sem.at[side])
         for side, ring in ((0, ring_y), (1, ring_x))
     ]
+    for i in (0, 1):
+        for side in (0, 1):
+            ring_middle(*whole(i, side))
     for side in (0, 1):
-        ring_start(*whole[side])
-    for side in (0, 1):
-        ring_middle(*whole[side])
-    for side in (0, 1):
-        ring_wait(s_second.at[side], sum_sem.at[side])
         me = (x0, y0)[side]
-        for z in (0, 1):
-            rest[side, :, z] = sums[side, me, z] + s_second[side, 0, z] + s_second[side, 1, z]
+        for i, (sums, first, second) in enumerate(steps):
+            ring_wait(second.at[side], sum_sem.at[i, side])
+            for z in (0, 1):
+                rest[side, :, z, i:2 * i + 1] = sums[side, me, z] + second[side, 0, z] + second[side, 1, z]
         ring_start(*part_of[side])
     for side in (0, 1):
         ring_middle(*part_of[side])
@@ -445,9 +473,12 @@
     return pl.pallas_call(
         update_kernel,
         out_shape=(tall, tall, small, small, small),
-        in_specs=[hbm, hbm, hbm, vmem, vmem, vmem, smem, smem],
+        in_specs=[hbm] * 6 + [smem, smem],
         out_specs=(vmem,) * 5,
         scratch_shapes=[
+            pltpu.VMEM((512, 512), F32),
+            pltpu.VMEM((512, 512), F32),
+            pltpu.VMEM((512, 512), F32),
             pltpu.VMEM((640, 2560), F32),
             pltpu.VMEM((640, 2560), BF16),
             pltpu.VMEM((640, 2560), BF16),
@@ -467,9 +498,12 @@
             pltpu.VMEM((2, 80, 512), F32),
             pltpu.VMEM((3, 128, 512), F32),
             pltpu.VMEM((2, 512, 512), BF16),
-            pltpu.VMEM((2, 4, 2, 4, 3, 16, 128), F32),
-            pltpu.VMEM((2, 2, 4, 3, 16, 128), F32),
-            pltpu.VMEM((2, 2, 2, 4, 3, 16, 128), F32),
+            pltpu.VMEM((2, 4, 2, 4, 1, 16, 128), F32),
+            pltpu.VMEM((2, 2, 4, 1, 16, 128), F32),
+            pltpu.VMEM((2, 2, 2, 4, 1, 16, 128), F32),
+            pltpu.VMEM((2, 4, 2, 4, 2, 16, 128), F32),
+            pltpu.VMEM((2, 2, 4, 2, 16, 128), F32),
+            pltpu.VMEM((2, 2, 2, 4, 2, 16, 128), F32),
             pltpu.VMEM((2, 4, 2, 3, 16, 128), F32),
             pltpu.VMEM((2, 2, 3, 16, 128), F32),
             pltpu.VMEM((2, 2, 2, 3, 16, 128), F32),
@@ -478,15 +512,15 @@
             pltpu.VMEM((2, 3, 16, 128), F32),
             pltpu.VMEM((3, 2, 3, 16, 128), F32),
             pltpu.VMEM((2, 4, 2, 3, 16, 128), F32),
-            dma((4,)),
-            dma((140,)),
+            dma((7,)),
+            dma((160,)),
             dma((4, 2, 4, 2)),
             dma((4, 6)),
             dma((4,)),
             dma((4, 4)),
             dma((4,)),
-            dma((2,)),
-            dma((2, 6)),
+            dma((3,)),
+            dma((2, 2, 6)),
             dma((2, 6)),
             dma((4,)),
             dma((2, 4)),

time: 131 us -> 127 us (0.969)
  Pallas kernels: 131 us -> 127 us
    pallas_call x1, Pallas kernels: 128 us -> 124 us  [update(): pl.pallas_call(update_kernel, out_shape=(tall, tall, small, small, small)...]
where the time goes in v4:
time: 127 us
  Pallas kernels  127 us (100%)
    pallas_call x1, Pallas kernels, update(): pl.pallas_call(update_kernel, out_shape=(tall, tall, small, small, small)...  124 us

profile of v4, /device:TPU:1, one launch (start us, length us, event | category | flops | bytes accessed | tf_op | source)
XLA Modules:
  0.0 127.1 jit_solution(7692857081400353839)
XLA Ops:
  0.6 124.4 %update.1 = (f32[80,512]{1,0:T(8,128)}, f32[80,512]{1,0:T(8,128)}, f32[64,512]{1,0:T(8,128)}, f32[64,512]{1,0:T(8,128)}, f32[64,512]{1,0:T(8,128)}) custom-call(f32[640,2560]{1,0:T(8,128)} %k_hbm.1, f32[16,2560]{1,0:T(8,128)} %bitcast.5, f32[16,2560]{1,0:T(8,128)} %bitcast.6, f32[512,512]{1,0:T(8,128)} %c_hbm.1, f32[512,512]{1,0:T(8,128)} %d_one_hbm.1, ...), custom_call_target="tpu_custom_call" | custom-call | tf_op jit(solution)/shard_map/update/pallas_call | solution.py:473
  125.1 2.1 %emit.1 = (f32[80,512]{1,0:T(8,128)}, f32[80,512]{1,0:T(8,128)}, f32[64,512]{1,0:T(8,128)}, f32[64,512]{1,0:T(8,128)}, f32[64,512]{1,0:T(8,128)}) custom-call(f32[80,512]{1,0:T(8,128)} %get-tuple-element.15.refs_0_, f32[80,512]{1,0:T(8,128)} %get-tuple-element.16.refs_1_, f32[64,512]{1,0:T(8,128)} %get-tuple-element.17.refs_2_, ...), custom_call_target="tpu_custom_call" | custom-call | tf_op jit(solution)/shard_map/emit/pallas_call | solution.py:542

commit v5 on v4

--- a/solution.py
+++ b/solution.py
@@ -50,7 +50,7 @@
     x1_out, x2_out, first_out, cross_out, second_out,
     coupling, diag_one, diag_two,
     k_f32, k_hi, k_lo, panels, mask, y, y_first, y_second, half_out, half_in, own, turned, y_two,
-    pieces, mate_pieces, blocks, mate_blocks, slices, c_split, sums_a, a_first, a_second, sums_b, b_first, b_second, rest, r_first, r_second,
+    pieces, mate_pieces, blocks, mate_blocks, slices, c_split, sums_a, a_first, a_second, sums_b, b_first, b_second, rest, r_in,
     z_pair, z_in, over_g, g_in, gathered,
     local_sem, send_sem, recv_sem, x_sem, z_sem, p_send, p_recv, mate_sem, sum_sem, rest_sem, tail_sem, end_sem,
 ):
@@ -67,6 +67,7 @@
     sibling = at(g0, y0, 1 - k0)
     x_up, x_down = (row, z0 * 4 + (x0 + 1) % 4), (row, z0 * 4 + (x0 + 3) % 4)
     y_far, g_far = at(g0, y0 + 2, k0), at(g0 + 2, y0, k0)
+    x_far = (row, z0 * 4 + (x0 + 2) % 4)
     z_mate = (row, (1 - z0) * 4 + x0)
     hands_out = g0 == col // 2
     level = (y0 // 2) == (col % 2)
@@ -91,7 +92,7 @@
         copy.start()
 
     barrier = pltpu.get_barrier_semaphore()
-    for device in (y_up, y_down, y_far, g_up, g_down, g_far, sibling, x_up, x_down, z_mate):
+    for device in (y_up, y_down, y_far, g_up, g_down, g_far, sibling, x_up, x_down, x_far, z_mate):
         pl.semaphore_signal(barrier, inc=1, device_id=device, device_id_type=MESH)
 
     @pl.when(hands_out)
@@ -106,7 +107,7 @@
         pl.semaphore_signal(barrier, inc=1, device_id=giver, device_id_type=MESH)
 
     extra = jnp.where(hands_out, 4, 0) + jnp.where(stays, -1, 1)
-    pl.semaphore_wait(barrier, 10 + extra)
+    pl.semaphore_wait(barrier, 11 + extra)
     for copy in firsts:
         copy.wait()
     squares = [
@@ -237,8 +238,6 @@
                 for i in range(4):
                     hand(i)
 
-        if t < 3:
-            hand_all()
         return hand_all
 
     def reduce_x(t):
@@ -293,7 +292,7 @@
     end_y(order[0])
     arrive(g0 + 1, 0, y0, k0)
     spread_y(order[1])
-    compute(0, order[0])
+    hand_0 = compute(0, order[0])
     for copy in squares:
         copy.wait()
     hi, lo = split(coupling[...])
@@ -308,19 +307,22 @@
     spread_y(order[2])
     ring_middle(*x_ring(0))
     end_y(order[1])
-    compute(1, order[1])
+    hand_1 = compute(1, order[1])
     reduce_x(0)
     relay_y(order[2])
     arrive(g0 + 2, 0, y0, k0)
     arrive(g0 + 2, 1, y0, k0)
     spread_y(order[3])
     ring_middle(*x_ring(1))
+    hand_0()
     end_y(order[2])
-    compute(2, order[2])
+    hand_2 = compute(2, order[2])
     reduce_x(1)
     finish_y(0, order[0])
     relay_y(order[3])
     ring_middle(*x_ring(2))
+    hand_1()
+    hand_2()
     diag_coupled = dot3(slices[0, mine, :], diag_one[...], ((1,), (1,)))
     end_y(order[3])
     hand_last = compute(3, order[3])
@@ -393,10 +395,7 @@
     place(sums_b, 1, later[:, 256:])
     for side in (0, 1):
         ring_start(*whole(1, side))
-    part_of = [
-        ((lambda w, z, side=side: rest.at[side, w, z]), *ring, r_first.at[side], r_second.at[side], rest_sem.at[side])
-        for side, ring in ((0, ring_y), (1, ring_x))
-    ]
+    mates = ((y_up, y_far, y_down), (x_up, x_far, x_down))
     for i in (0, 1):
         for side in (0, 1):
             ring_middle(*whole(i, side))
@@ -406,14 +405,15 @@
             ring_wait(second.at[side], sum_sem.at[i, side])
             for z in (0, 1):
                 rest[side, :, z, i:2 * i + 1] = sums[side, me, z] + second[side, 0, z] + second[side, 1, z]
-        ring_start(*part_of[side])
+        other = (y0, x0)[side]
+        for d in (2, 1, 3):
+            send(rest.at[side, (other + d) % 4], r_in.at[side, d - 1], rest_sem.at[side, d - 1], mates[side][d - 1])
     for side in (0, 1):
-        ring_middle(*part_of[side])
-    for side in (0, 1):
-        ring_wait(r_second.at[side], rest_sem.at[side])
         me = (y0, x0)[side]
+        for d in range(3):
+            landed(r_in.at[side, d], rest_sem.at[side, d])
         for z in (0, 1):
-            z_pair[z, side] = rest[side, me, z] + r_second[side, 0, z] + r_second[side, 1, z]
+            z_pair[z, side] = (rest[side, me, z] + r_in[side, 0, z]) + (r_in[side, 1, z] + r_in[side, 2, z])
     send(z_pair.at[1 - z0], z_in, tail_sem.at[0], z_mate)
     landed(z_in, tail_sem.at[0])
     over_g[...] = z_pair[z0] + z_in[...]
@@ -505,8 +505,7 @@
             pltpu.VMEM((2, 2, 4, 2, 16, 128), F32),
             pltpu.VMEM((2, 2, 2, 4, 2, 16, 128), F32),
             pltpu.VMEM((2, 4, 2, 3, 16, 128), F32),
-            pltpu.VMEM((2, 2, 3, 16, 128), F32),
-            pltpu.VMEM((2, 2, 2, 3, 16, 128), F32),
+            pltpu.VMEM((2, 3, 2, 3, 16, 128), F32),
             pltpu.VMEM((2, 2, 3, 16, 128), F32),
             pltpu.VMEM((2, 3, 16, 128), F32),
             pltpu.VMEM((2, 3, 16, 128), F32),

time: 127 us -> 126 us (level)
  Pallas kernels: 127 us -> 125 us
    pallas_call x1, Pallas kernels: 124 us -> 123 us  [update(): pl.pallas_call(update_kernel, out_shape=(tall, tall, small, small, small)...]
where the time goes in v5:
time: 126 us
  Pallas kernels  125 us (99%)
    pallas_call x1, Pallas kernels, update(): pl.pallas_call(update_kernel, out_shape=(tall, tall, small, small, small)...  123 us

profile of v5, /device:TPU:1, one launch (start us, length us, event | category | flops | bytes accessed | tf_op | source)
XLA Modules:
  0.0 125.8 jit_solution(4744411905362961578)
XLA Ops:
  0.6 123.1 %update.1 = (f32[80,512]{1,0:T(8,128)}, f32[80,512]{1,0:T(8,128)}, f32[64,512]{1,0:T(8,128)}, f32[64,512]{1,0:T(8,128)}, f32[64,512]{1,0:T(8,128)}) custom-call(f32[640,2560]{1,0:T(8,128)} %k_hbm.1, f32[16,2560]{1,0:T(8,128)} %bitcast.5, f32[16,2560]{1,0:T(8,128)} %bitcast.6, f32[512,512]{1,0:T(8,128)} %c_hbm.1, f32[512,512]{1,0:T(8,128)} %d_one_hbm.1, ...), custom_call_target="tpu_custom_call" | custom-call | tf_op jit(solution)/shard_map/update/pallas_call | solution.py:473
  123.7 2.1 %emit.1 = (f32[80,512]{1,0:T(8,128)}, f32[80,512]{1,0:T(8,128)}, f32[64,512]{1,0:T(8,128)}, f32[64,512]{1,0:T(8,128)}, f32[64,512]{1,0:T(8,128)}) custom-call(f32[80,512]{1,0:T(8,128)} %get-tuple-element.15.refs_0_, f32[80,512]{1,0:T(8,128)} %get-tuple-element.16.refs_1_, f32[64,512]{1,0:T(8,128)} %get-tuple-element.17.refs_2_, ...), custom_call_target="tpu_custom_call" | custom-call | tf_op jit(solution)/shard_map/emit/pallas_call | solution.py:541
